TPU v7x, 256 devices: a whole 4x4x8 slice. The times are simulated.
256 devices in a mesh: section: 32 (over x, z), expert: 8 (over y, core).
Axes of the slice: x: 4, y: 4, z: 8, core: 2. Of those that a mesh axis runs over, the one named last changes fastest.
Arguments:
- tokens: bfloat16 [2048, 4096], P('expert', 'section'), may hold values from -6 to 6
- routes: int32 [2048, 2], P('expert'), may hold values from 0 to 7, all different within a row; in each aligned block of 256 rows (0 to 255, 256 to 511, ...) at most 80 rows name the same one
- mix_weights: float32 [2048, 2], P('expert'), may hold values from 0.2 to 1
- w_gate: bfloat16 [8, 4096, 8192], P('expert', None, 'section'), may hold values from -0.1875 to 0.1875
- w_up: bfloat16 [8, 4096, 8192], P('expert', None, 'section'), may hold values from -0.1875 to 0.1875
- w_down: bfloat16 [8, 8192, 4096], P('expert', 'section'), may hold values from -0.125 to 0.125
- upstream: bfloat16 [2048, 4096], P('expert', 'section'), may hold values from -6 to 6
Outputs:
- mixed: bfloat16 [2048, 4096], P('expert', 'section')
- grad_tokens: bfloat16 [2048, 4096], P('expert', 'section')
- grad_mix: float32 [2048, 2], P('expert')
- grad_gate: bfloat16 [8, 4096, 8192], P('expert', None, 'section')
- grad_up: bfloat16 [8, 4096, 8192], P('expert', None, 'section')
- grad_down: bfloat16 [8, 8192, 4096], P('expert', 'section')
Inputs may be any that keep to these rules, and one draw needn't show every extreme that they name: `routes`: each token names 2 different experts. Among the 256 tokens of one index of the expert axis no expert is named more than 80 times, and in some such block one expert is named exactly 80 times.
All inputs are finite; a program needn't handle non-finite values.
Results may differ from a plain program's by a relative error of at most 0.02.
Values may be sent and summed in bfloat16 or wider, within the bound.
No kernel may reach another device: no remote copies, remote signals or barrier semaphores. Data moves between devices by JAX's collectives and lax.ppermute only.
A program may use at most 128 MiB of HBM per device.

v0:
```python
import jax
import jax.numpy as jnp
from jax import lax
from jax.sharding import PartitionSpec as P

highest = lax.Precision.HIGHEST


def slot_tables(route_rows, mix_rows, capacity, experts):
    tok_count, top_count = route_rows.shape
    flat_routes = route_rows.reshape(-1)
    onehot = (flat_routes[:, None] == jnp.arange(experts, dtype=jnp.int32)[None, :]).astype(
        jnp.int32
    )
    earlier = jnp.cumsum(onehot, axis=0) - onehot
    position = jnp.sum(earlier * onehot, axis=1)
    target = (flat_routes * capacity + position).reshape(tok_count, top_count)
    slot_ids = jnp.arange(experts * capacity, dtype=jnp.int32)
    hits = target[None, :, :] == slot_ids[:, None, None]
    matches = hits.astype(jnp.float32)
    select = jnp.sum(matches, axis=2)
    weighted = jnp.sum(matches * mix_rows[None, :, :], axis=2)
    token_ids = jnp.arange(tok_count, dtype=jnp.int32)
    slot_token = jnp.sum(jnp.sum(hits.astype(jnp.int32), axis=2) * token_ids[None, :], axis=1)
    return (target, select, weighted, slot_token)


def per_device(tokens, routes, mix_weights, w_gate, w_up, w_down, upstream):
    experts = lax.axis_size("expert")
    tok_count = tokens.shape[0]
    top_count = routes.shape[1]
    capacity = 5 * tok_count * top_count // (4 * experts)
    slot_total = experts * capacity
    target, select, weighted, slot_token = slot_tables(routes, mix_weights, capacity, experts)
    slot_fill = jnp.sum(select, axis=1)
    slot_scale = jnp.sum(weighted, axis=1)
    gate_local = w_gate[0]
    up_local = w_up[0]
    down_local = w_down[0]

    def collect(source, factor):
        taken = source[slot_token].astype(jnp.float32)
        return (taken * factor[:, None]).astype(jnp.bfloat16)

    def to_experts(source, factor):
        block = collect(source, factor)
        arrived = lax.all_to_all(
            block.reshape(experts, capacity, -1), "expert", split_axis=0, concat_axis=0, tiled=True
        )
        whole = lax.all_gather(arrived, "section", axis=2, tiled=True)
        return whole.reshape(slot_total, -1)

    def to_sources(partial_value):
        summed = lax.psum_scatter(
            partial_value.reshape(experts, capacity, -1).astype(jnp.bfloat16),
            "section",
            scatter_dimension=2,
            tiled=True,
        )
        back = lax.all_to_all(summed, "expert", split_axis=0, concat_axis=0, tiled=True)
        return back.reshape(slot_total, -1)

    dispatched = to_experts(tokens, slot_fill)
    act_gate = jnp.dot(dispatched, gate_local, preferred_element_type=jnp.float32)
    act_up = jnp.dot(dispatched, up_local, preferred_element_type=jnp.float32)
    sig = jax.nn.sigmoid(act_gate)
    silu_gate = act_gate * sig
    hidden = (silu_gate * act_up).astype(jnp.bfloat16)
    partial_value = jnp.dot(hidden, down_local, preferred_element_type=jnp.float32)
    returned = to_sources(partial_value).astype(jnp.float32)
    moe_out = jnp.dot(weighted.T, returned, precision=highest)
    mixed = (tokens.astype(jnp.float32) + moe_out).astype(jnp.bfloat16)
    picked = returned[target]
    upstream_wide = upstream.astype(jnp.float32)
    mix_terms = jnp.einsum("tkd,td->tk", picked, upstream_wide, precision=highest)
    grad_mix = lax.psum(mix_terms, "section")
    grad_rows = to_experts(upstream, slot_scale)
    grad_hidden = lax.dot_general(
        grad_rows, down_local, (((1,), (1,)), ((), ())), preferred_element_type=jnp.float32
    )
    grad_down = lax.dot_general(
        hidden, grad_rows, (((0,), (0,)), ((), ())), preferred_element_type=jnp.float32
    ).astype(jnp.bfloat16)
    dsilu = sig * (1.0 + act_gate * (1.0 - sig))
    grad_act_gate = (grad_hidden * act_up * dsilu).astype(jnp.bfloat16)
    grad_act_up = (grad_hidden * silu_gate).astype(jnp.bfloat16)
    grad_gate = lax.dot_general(
        dispatched, grad_act_gate, (((0,), (0,)), ((), ())), preferred_element_type=jnp.float32
    ).astype(jnp.bfloat16)
    grad_up = lax.dot_general(
        dispatched, grad_act_up, (((0,), (0,)), ((), ())), preferred_element_type=jnp.float32
    ).astype(jnp.bfloat16)
    first = lax.dot_general(
        grad_act_gate, gate_local, (((1,), (1,)), ((), ())), preferred_element_type=jnp.float32
    )
    second = lax.dot_general(
        grad_act_up, up_local, (((1,), (1,)), ((), ())), preferred_element_type=jnp.float32
    )
    back_rows = to_sources(first + second).astype(jnp.float32)
    grad_moe = jnp.dot(select.T, back_rows, precision=highest)
    grad_tokens = (upstream_wide + grad_moe).astype(jnp.bfloat16)
    return (mixed, grad_tokens, grad_mix, grad_gate[None], grad_up[None], grad_down[None])


def solution(mesh):
    return jax.shard_map(
        per_device,
        mesh=mesh,
        in_specs=(
            P("expert", "section"),
            P("expert", None),
            P("expert", None),
            P("expert", None, "section"),
            P("expert", None, "section"),
            P("expert", "section", None),
            P("expert", "section"),
        ),
        out_specs=(
            P("expert", "section"),
            P("expert", "section"),
            P("expert", None),
            P("expert", None, "section"),
            P("expert", None, "section"),
            P("expert", "section", None),
        ),
        check_vma=False,
    )
```

profile of v0, /device:TPU:8, one launch (start us, length us, event | category | flops | bytes accessed | tf_op | source)
XLA Modules:
  0.0 783.5 jit_solution(15971595313948356913)
XLA Ops:
  11.4 2.1 select_reduce_fusion
  15.7 10.3 %all_to_all.20 = bf16[8,80,128]{2,1,0:T(8,128)(2,1)} all-to-all(bf16[8,80,128]{2,1,0:T(8,128)(2,1)S(1)} %fusion.17), channel_id=1, replica_groups=mesh['section'=32,'expert'=8] {'expert'}, dimensions={0} | all-to-all | bytes 327680 | tf_op jit(solution)/shard_map/all_to_all | solution.py:47
  28.3 9.5 %all_to_all.21 = bf16[8,80,128]{2,1,0:T(8,128)(2,1)} all-to-all(bf16[8,80,128]{2,1,0:T(8,128)(2,1)S(1)} %fusion.16), channel_id=1, replica_groups=mesh['section'=32,'expert'=8] {'expert'}, dimensions={0} | all-to-all | bytes 327680 | tf_op jit(solution)/shard_map/all_to_all | solution.py:47
  37.9 77.2 %all-gather.3.cloned.1.call-done = bf16[8,80,4096]{2,1,0:T(8,128)(2,1)} async-done(((bf16[8,80,128]{2,1,0:T(8,128)(2,1)}), bf16[8,80,4096]{2,1,0:T(8,128)(2,1)}) %all-gather.3.cloned.1.call-update) | async-done | bytes 5242896 | tf_op jit(solution)/shard_map/all_gather | solution.py:50
  115.2 5.7 fusion.7
  120.8 2.4 fusion.11
  123.2 81.6 %all-gather.5.cloned.1.call-done = bf16[8,80,4096]{2,1,0:T(8,128)(2,1)} async-done(((bf16[8,80,128]{2,1,0:T(8,128)(2,1)}), bf16[8,80,4096]{2,1,0:T(8,128)(2,1)}) %all-gather.5.cloned.1.call-update) | async-done | bytes 5242896 | tf_op jit(solution)/shard_map/all_gather | solution.py:50
  204.7 5.4 multiply_convert_fusion
  210.1 3.9 convolution_convert_fusion
  214.0 11.2 %copy.36 = bf16[8,80,4096]{1,0,2:T(8,128)(2,1)} copy(bf16[8,80,4096]{2,1,0:T(8,128)(2,1)} %convolution_convert_fusion) | data formatting | bytes 10485760
  225.2 13.1 %reshape.124 = bf16[4096,640]{1,0:T(8,128)(2,1)} reshape(bf16[4096,8,80]{2,1,0:T(8,128)(2,1)} %bitcast.66) | data formatting | bytes 10485760
  239.8 2.7 fusion.9
  242.5 3.9 add_convert_fusion
  246.4 11.2 %copy.38 = bf16[8,80,4096]{1,0,2:T(8,128)(2,1)} copy(bf16[8,80,4096]{2,1,0:T(8,128)(2,1)} %bitcast.69) | data formatting | bytes 10485760
  257.6 13.1 %reshape.126 = bf16[4096,640]{1,0:T(8,128)(2,1)} reshape(bf16[4096,8,80]{2,1,0:T(8,128)(2,1)} %bitcast.67) | data formatting | bytes 10485760
  271.7 5.7 fusion.1
  277.4 5.8 fusion
  283.2 180.6 %reduce-scatter.7.cloned.1.call-done = bf16[128,640]{1,0:T(8,128)(2,1)} async-done(((bf16[4096,640]{1,0:T(8,128)(2,1)}), bf16[128,640]{1,0:T(8,128)(2,1)}) %reduce-scatter.7.cloned.1.call-update) | async-done | bytes 163856
  465.8 4.8 all-to-all-start.1
  470.6 5.8 fusion.2
  476.4 215.3 %reduce-scatter.9.cloned.1.call-done = bf16[128,640]{1,0:T(8,128)(2,1)} async-done(((bf16[4096,640]{1,0:T(8,128)(2,1)}), bf16[128,640]{1,0:T(8,128)(2,1)}) %reduce-scatter.9.cloned.1.call-update) | async-done | bytes 163856
  693.7 4.8 all-to-all-start.3
  700.3 72.8 %psum.7 = f32[256,2]{0,1:T(2,128)} all-reduce(f32[256,2]{0,1:T(2,128)S(1)} %bitcast.81), channel_id=1, replica_groups=mesh['section'=32,'expert'=8] {'section'}, use_global_device_ids=true, to_apply=%region_11.12 | all-reduce | flops 512 | bytes 4096 | tf_op jit(solution)/shard_map/psum | solution.py:76
  773.2 2.4 fusion.13
  (65 shorter events, 18.5 us)
Async XLA Ops:
  7.2 197.6 %copy-start = (bf16[1,256,4096]{2,1,0:T(8,128)(2,1)S(1)}, bf16[1,256,4096]{2,1,0:T(8,128)(2,1)}, u32[]{:S(2)}) copy-start(bf16[1,256,4096]{2,1,0:T(8,128)(2,1)} %param.12) | copy-start | bytes 6291460
  7.2 6.4 copy-start.2
  7.2 18.9 %copy-start.3 = (bf16[256,128]{1,0:T(8,128)(2,1)S(1)}, bf16[256,128]{1,0:T(8,128)(2,1)}, u32[]{:S(2)}) copy-start(bf16[256,128]{1,0:T(8,128)(2,1)} %param.13) | copy-start | bytes 196612
  7.2 108.0 %all-gather.3.cloned.1.call-start = ((), (), s32[]{:S(2)}) async-start(), calls=%async_computation.6 | async-start | bytes 5406720 | tf_op jit(solution)/shard_map/all_gather | solution.py:50
  26.0 178.7 %all-gather.5.cloned.1.call-start = ((), (), s32[]{:S(2)}) async-start(), calls=%async_computation.7 | async-start | bytes 5406720 | tf_op jit(solution)/shard_map/all_gather | solution.py:50
  37.9 425.9 %reduce-scatter.7.cloned.1.call-start = ((), (), s32[]{:S(2)}) async-start(), calls=%async_computation.8 | async-start | bytes 5406720
  115.2 5.7 copy-start.4
  115.2 5.7 copy-start.10
  238.2 1.6 copy-start.5
  238.3 453.4 %reduce-scatter.9.cloned.1.call-start = ((), (), s32[]{:S(2)}) async-start(), calls=%async_computation.9 | async-start | bytes 5406720
  239.8 2.7 copy-start.6
  239.8 2.7 copy-start.8
  270.7 1.0 copy-start.9
  271.7 5.7 copy-start.7
  465.8 227.9 %all-to-all-start.1 = ((bf16[8,80,128]{2,1,0:T(8,128)(2,1)}), bf16[8,80,128]{2,1,0:T(8,128)(2,1)S(1)}, u32[]{:S(2)}, u32[]{:S(2)}) async-start(bf16[8,80,128]{2,1,0:T(8,128)(2,1)} %copy.37), calls=%async_computation.1 | async-start | bytes 327680 | tf_op jit(solution)/shard_map/all_to_all | solution.py:60
  470.6 306.3 %copy-start.1 = (bf16[1,256,4096]{2,1,0:T(8,128)(2,1)S(1)}, bf16[1,256,4096]{2,1,0:T(8,128)(2,1)}, u32[]{:S(2)}) copy-start(bf16[1,256,4096]{2,1,0:T(8,128)(2,1)} %param.12) | copy-start | bytes 6291460
  693.7 81.9 %all-to-all-start.3 = ((bf16[8,80,128]{2,1,0:T(8,128)(2,1)}), bf16[8,80,128]{2,1,0:T(8,128)(2,1)S(1)}, u32[]{:S(2)}, u32[]{:S(2)}) async-start(bf16[8,80,128]{2,1,0:T(8,128)(2,1)} %copy.39), calls=%async_computation.3 | async-start | bytes 327680 | tf_op jit(solution)/shard_map/all_to_all | solution.py:60
Sparse Core Ops, SparseCore 0:
  26.1 88.9 all-gather.2
  117.6 87.0 all-gather.4
  238.4 225.3 reduce-scatter.6
  467.6 224.0 reduce-scatter.8
where the time goes:
time: 785 us; the launch traced here: 783 us
  waiting for transfers between devices  555 us (71%)
  blocking collectives  92.6 us (12%)
  local copies, waits for them, and re-layouts  62.1 us (8%)
  matrix products  45.3 us (6%)
  between operations  14 us (2%)
  starting transfers between devices  9.93 us (1%)
    unnamed x6, waiting for transfers between devices  396 us
    all_gather x2, waiting for transfers between devices, to_experts(): whole = lax.all_gather(arrived, 'section', axis=2, tiled=True)  159 us
    psum x1, blocking collectives, per_device(): grad_mix = lax.psum(mix_terms, 'section')  72.8 us
    unnamed x31, local copies, waits for them, and re-layouts  55.6 us
    all_to_all x2, blocking collectives, to_experts(): lax.all_to_all(block.reshape(experts, capacity, -1), 'expert', split_axis...  19.8 us
  transfers between devices with their start and end apart: 6, of which 4 were waited for; matrix products, arithmetic and copies ran while one was open for 9% of the time, Pallas kernels for 0%

commit v1 on v0

--- a/solution.py
+++ b/solution.py
@@ -47,7 +47,9 @@
         arrived = lax.all_to_all(
             block.reshape(experts, capacity, -1), "expert", split_axis=0, concat_axis=0, tiled=True
         )
-        whole = lax.all_gather(arrived, "section", axis=2, tiled=True)
+        whole = jnp.concatenate(
+            lax.all_to_all(jnp.stack([arrived] * lax.axis_size("section")), "section", 0, 0), axis=2
+        )
         return whole.reshape(slot_total, -1)
 
     def to_sources(partial_value):

time: 785 us -> 885 us (1.13)
  blocking collectives: 92.6 us -> 211 us
  waiting for transfers between devices: 555 us -> 501 us
  local copies, waits for them, and re-layouts: 62.1 us -> 83.7 us
  starting transfers between devices: 9.93 us -> 21 us
    all_gather x2 -> x0, waiting for transfers between devices: 159 us -> none  [to_experts(): whole = lax.all_gather(arrived, 'section', axis=2, tiled=True)]
    all_to_all x0 -> x1, blocking collectives: none -> 129 us  [to_experts(): lax.all_to_all(jnp.stack([arrived] * lax.axis_size('section')), 'section'...]
    all_to_all x0 -> x2, waiting for transfers between devices: none -> 113 us  [the longest x1 110 us: to_experts(): lax.all_to_all(jnp.stack([arrived] * lax.axis_size('section')), 'section'...]
    reshape x0 -> x2, local copies, waits for them, and re-layouts: none -> 14.3 us  [to_experts(): jnp.concatenate(lax.all_to_all(jnp.stack([arrived] * lax.axis_size('secti...]
    all_to_all x2 -> x1, blocking collectives: 19.8 us -> 8.86 us  [to_experts(): lax.all_to_all(block.reshape(experts, capacity, -1), 'expert', split_axis...]
    all_to_all x0 -> x2, starting transfers between devices: none -> 10.5 us  [the longest x1 5.48 us: to_experts(): lax.all_to_all(block.reshape(experts, capacity, -1), 'expert', split_axis...]
    unnamed x6 -> x4, waiting for transfers between devices: 396 us -> 388 us
    unnamed x31 -> x45, local copies, waits for them, and re-layouts: 55.6 us -> 57.7 us
  transfers between devices with their start and end apart: 6 -> 6, of which waited for: 4 -> 4; matrix products, arithmetic and copies ran while one was open for 9% -> 8% of each run, Pallas kernels for 0% -> 0%
where the time goes in v1:
time: 885 us; the launch traced here: 878 us
  waiting for transfers between devices  501 us (57%)
  blocking collectives  211 us (24%)
  local copies, waits for them, and re-layouts  83.7 us (9%)
  matrix products  41.7 us (5%)
  starting transfers between devices  21 us (2%)
  between operations  14.7 us (2%)
    unnamed x4, waiting for transfers between devices  388 us
    all_to_all x1, blocking collectives, to_experts(): lax.all_to_all(jnp.stack([arrived] * lax.axis_size('section')), 'section'...  129 us
    all_to_all x1, waiting for transfers between devices, to_experts(): lax.all_to_all(jnp.stack([arrived] * lax.axis_size('section')), 'section'...  110 us
    psum x1, blocking collectives, per_device(): grad_mix = lax.psum(mix_terms, 'section')  72.9 us
    unnamed x45, local copies, waits for them, and re-layouts  57.7 us
  transfers between devices with their start and end apart: 6, of which 4 were waited for; matrix products, arithmetic and copies ran while one was open for 8% of the time, Pallas kernels for 0%

profile of v1, /device:TPU:8, one launch (start us, length us, event | category | flops | bytes accessed | tf_op | source)
XLA Modules:
  0.0 878.5 jit_solution(14500645729859562221)
XLA Ops:
  13.8 2.6 gather_fusion
  17.2 5.5 all-to-all-start
  24.9 2.8 all-to-all-done
  27.7 8.9 %all_to_all.30 = bf16[8,80,128]{2,1,0:T(8,128)(2,1)S(1)} all-to-all(bf16[8,80,128]{2,1,0:T(8,128)(2,1)S(1)} %fusion.46), channel_id=1, replica_groups=mesh['section'=32,'expert'=8] {'expert'}, dimensions={0} | all-to-all | bytes 327680 | tf_op jit(solution)/shard_map/all_to_all | solution.py:47
  37.7 129.1 %all_to_all.31 = bf16[32,8,80,128]{3,2,1,0:T(8,128)(2,1)} all-to-all(bf16[32,8,80,128]{3,2,1,0:T(8,128)(2,1)S(1)} %stack.5), channel_id=1, replica_groups=mesh['section'=32,'expert'=8] {'section'}, dimensions={0} | all-to-all | bytes 10485760 | tf_op jit(solution)/shard_map/all_to_all | solution.py:51
  166.8 3.5 stack.4
  170.3 5.1 all-to-all-start.1
  175.9 8.2 copy.38
  184.2 109.8 %all-to-all-done.1 = bf16[32,8,80,128]{3,2,1,0:T(8,128)(2,1)} async-done(((bf16[32,8,80,128]{3,2,1,0:T(8,128)(2,1)}), bf16[32,8,80,128]{3,2,1,0:T(8,128)(2,1)}, u32[]{:S(2)}, u32[]{:S(2)}) %all-to-all-start.1) | async-done | bytes 5242912 | tf_op jit(solution)/shard_map/all_to_all | solution.py:51
  294.0 6.0 copy.37
  307.6 3.9 convolution_convert_fusion
  311.5 11.2 %copy.42 = bf16[8,80,4096]{1,0,2:T(8,128)(2,1)} copy(bf16[8,80,4096]{2,1,0:T(8,128)(2,1)} %convolution_convert_fusion) | data formatting | bytes 10485760
  322.6 13.1 %reshape.128 = bf16[4096,640]{1,0:T(8,128)(2,1)} reshape(bf16[4096,8,80]{2,1,0:T(8,128)(2,1)} %bitcast.92) | data formatting | bytes 10485760
  338.9 4.0 add_convert_fusion
  342.9 11.2 %copy.44 = bf16[8,80,4096]{1,0,2:T(8,128)(2,1)} copy(bf16[8,80,4096]{2,1,0:T(8,128)(2,1)} %bitcast.100) | data formatting | bytes 10485760
  354.1 13.3 %reshape.130 = bf16[4096,640]{1,0:T(8,128)(2,1)} reshape(bf16[4096,8,80]{2,1,0:T(8,128)(2,1)} %bitcast.93) | data formatting | bytes 10485760
  368.4 9.5 %fusion.24 = bf16[1,4096,256]{2,1,0:T(8,128)(2,1)} fusion(bf16[640,256]{1,0:T(8,128)(2,1)S(1)} %copy-done.13, bf16[80,8,32,128]{3,2,1,0:T(8,128)(2,1)} %bitcast.105), kind=kOutput, calls=%fused_computation.21 | convolution fusion | flops 1343225856 | bytes 7667712 | tf_op jit(solution)/shard_map/dot_general | solution.py:92
  377.8 6.8 fusion.27
  384.6 173.9 %reduce-scatter.7.cloned.1.call-done = bf16[128,640]{1,0:T(8,128)(2,1)} async-done(((bf16[4096,640]{1,0:T(8,128)(2,1)}), bf16[128,640]{1,0:T(8,128)(2,1)}) %reduce-scatter.7.cloned.1.call-update) | async-done | bytes 163856
  560.5 5.1 all-to-all-start.2
  565.6 6.1 fusion.21
  571.7 214.4 %reduce-scatter.9.cloned.1.call-done = bf16[128,640]{1,0:T(8,128)(2,1)} async-done(((bf16[4096,640]{1,0:T(8,128)(2,1)}), bf16[128,640]{1,0:T(8,128)(2,1)}) %reduce-scatter.9.cloned.1.call-update) | async-done | bytes 163856
  788.1 4.8 all-to-all-start.5
  794.7 72.9 %psum.7 = f32[256,2]{0,1:T(2,128)} all-reduce(f32[256,2]{0,1:T(2,128)S(1)} %bitcast.116), channel_id=1, replica_groups=mesh['section'=32,'expert'=8] {'section'}, use_global_device_ids=true, to_apply=%region_11.12 | all-reduce | flops 512 | bytes 4096 | tf_op jit(solution)/shard_map/psum | solution.py:78
  (83 shorter events, 32.6 us)
Async XLA Ops:
  7.2 297.7 %copy-start = (bf16[1,256,4096]{2,1,0:T(8,128)(2,1)S(1)}, bf16[1,256,4096]{2,1,0:T(8,128)(2,1)}, u32[]{:S(2)}) copy-start(bf16[1,256,4096]{2,1,0:T(8,128)(2,1)} %param.12) | copy-start | bytes 6291460
  7.2 15.5 %copy-start.3 = (bf16[256,128]{1,0:T(8,128)(2,1)S(1)}, bf16[256,128]{1,0:T(8,128)(2,1)}, u32[]{:S(2)}) copy-start(bf16[256,128]{1,0:T(8,128)(2,1)} %param.13) | copy-start | bytes 196612
  17.2 10.5 %all-to-all-start = ((bf16[8,80,128]{2,1,0:T(8,128)(2,1)}), bf16[8,80,128]{2,1,0:T(8,128)(2,1)S(1)}, u32[]{:S(2)}, u32[]{:S(2)}) async-start(bf16[8,80,128]{2,1,0:T(8,128)(2,1)} %fusion.47), calls=%async_computation | async-start | bytes 327680 | tf_op jit(solution)/shard_map/all_to_all | solution.py:47
  170.3 123.7 %all-to-all-start.1 = ((bf16[32,8,80,128]{3,2,1,0:T(8,128)(2,1)}), bf16[32,8,80,128]{3,2,1,0:T(8,128)(2,1)}, u32[]{:S(2)}, u32[]{:S(2)}) async-start(bf16[32,8,80,128]{3,2,1,0:T(8,128)(2,1)} %stack.4), calls=%async_computation.1 | async-start | bytes 10485760 | tf_op jit(solution)/shard_map/all_to_all | solution.py:51
  175.3 383.1 %reduce-scatter.7.cloned.1.call-start = ((), (), s32[]{:S(2)}) async-start(), calls=%async_computation.8 | async-start | bytes 5406720
  294.0 6.0 copy-start.8
  300.0 2.8 copy-start.4
  300.0 3.2 copy-start.6
  300.0 4.9 slice-start
  303.2 2.0 slice-start.1
  307.6 28.2 %copy-start.10 = (bf16[640,256]{1,0:T(8,128)(2,1)}, bf16[640,256]{1,0:T(8,128)(2,1)S(1)}, u32[]{:S(2)}) copy-start(bf16[640,256]{1,0:T(8,128)(2,1)S(1)} %get-tuple-element.13) | copy-start | bytes 983044
  307.6 31.3 %copy-start.12 = (bf16[640,256]{1,0:T(8,128)(2,1)}, bf16[640,256]{1,0:T(8,128)(2,1)S(1)}, u32[]{:S(2)}) copy-start(bf16[640,256]{1,0:T(8,128)(2,1)S(1)} %get-tuple-element.12) | copy-start | bytes 983044
  335.7 1.6 copy-start.7
  335.8 450.3 %reduce-scatter.9.cloned.1.call-start = ((), (), s32[]{:S(2)}) async-start(), calls=%async_computation.9 | async-start | bytes 5406720
  337.3 1.6 copy-start.9
  367.4 1.0 copy-start.13
  367.4 10.4 %slice-start.2 = ((s8[5242880]{0:T(1024)(128)(4,1)}), s8[1048576]{0:T(1024)(128)(4,1)S(1)}, s32[]{:S(2)}) async-start(s8[5242880]{0:T(1024)(128)(4,1)} %bitcast.106), calls=%async_computation.12 | async-start | bytes 2097152
  368.4 9.5 %slice-start.3 = ((s8[5242880]{0:T(1024)(128)(4,1)}), s8[4194304]{0:T(1024)(128)(4,1)S(1)}, s32[]{:S(2)}) async-start(s8[5242880]{0:T(1024)(128)(4,1)} %bitcast.106), calls=%async_computation.13 | async-start | bytes 8388608
  368.4 9.5 %copy-start.11 = (bf16[640,256]{1,0:T(8,128)(2,1)S(1)}, bf16[640,256]{1,0:T(8,128)(2,1)}, u32[]{:S(2)}) copy-start(bf16[640,256]{1,0:T(8,128)(2,1)} %copy-done.10) | copy-start | bytes 983044
  560.5 227.6 %all-to-all-start.2 = ((bf16[8,80,128]{2,1,0:T(8,128)(2,1)}), bf16[8,80,128]{2,1,0:T(8,128)(2,1)S(1)}, u32[]{:S(2)}, u32[]{:S(2)}) async-start(bf16[8,80,128]{2,1,0:T(8,128)(2,1)} %copy.43), calls=%async_computation.2 | async-start | bytes 327680 | tf_op jit(solution)/shard_map/all_to_all | solution.py:62
  565.6 302.0 %copy-start.2 = (bf16[256,128]{1,0:T(8,128)(2,1)S(1)}, bf16[256,128]{1,0:T(8,128)(2,1)}, u32[]{:S(2)}) copy-start(bf16[256,128]{1,0:T(8,128)(2,1)} %param.7) | copy-start | bytes 196612
  565.6 304.4 %copy-start.5 = (f32[640,256]{1,0:T(8,128)S(1)}, f32[640,256]{1,0:T(8,128)}, u32[]{:S(2)}) copy-start(f32[640,256]{1,0:T(8,128)} %get-tuple-element.9) | copy-start | bytes 1966084
  565.6 305.8 %copy-start.1 = (bf16[1,256,4096]{2,1,0:T(8,128)(2,1)S(1)}, bf16[1,256,4096]{2,1,0:T(8,128)(2,1)}, u32[]{:S(2)}) copy-start(bf16[1,256,4096]{2,1,0:T(8,128)(2,1)} %param.12) | copy-start | bytes 6291460
  788.1 81.9 %all-to-all-start.5 = ((bf16[8,80,128]{2,1,0:T(8,128)(2,1)}), bf16[8,80,128]{2,1,0:T(8,128)(2,1)S(1)}, u32[]{:S(2)}, u32[]{:S(2)}) async-start(bf16[8,80,128]{2,1,0:T(8,128)(2,1)} %copy.45), calls=%async_computation.5 | async-start | bytes 327680 | tf_op jit(solution)/shard_map/all_to_all | solution.py:62
Sparse Core Ops, SparseCore 0:
  335.9 222.5 reduce-scatter.6
  562.4 223.6 reduce-scatter.8
